TPU v7x, 512 devices: a whole 4x4x16 slice. The times are simulated.
512 devices in a mesh: blk: 8 (over y_lo, x), rows: 64 (over z, y_hi, core).
Axes of the slice: x: 4, y: 4 (y_hi: 2, y_lo: 2; y = y_hi * 2 + y_lo), z: 16, core: 2. Of those that a mesh axis runs over, the one named last changes fastest.
Arguments:
- queries: bfloat16 [128, 4, 8192], P('rows', None, 'blk'), may hold values from -36 to 36
- new_entries: bfloat16 [128, 4, 2, 1024], P('rows', None, None, 'blk'), may hold values from -9 to 9
- resident: bfloat16 [4096, 2, 16, 1024], P('rows', None, None, 'blk'), may hold values from -9 to 9
- swap_area: bfloat16 [4096, 2, 16, 1024], P('rows', None, None, 'blk'), may hold values from -9 to 9
- swap_dest: int32 [4096], P('rows'), may hold values from 0 to 63, as said below
- page_table: int32 [128, 64], P('rows'), may hold values from 0 to 191, as said below
- lengths: int32 [128], P('rows'), may hold values from 256 to 1024, as said below
- norm_gain: bfloat16 [8192], P('blk'), may hold values from 0.099609375 to 1.8984375
- gate_weight: bfloat16 [8192, 28672], P('blk', 'rows'), may hold values from -0.0625 to 0.0625
- up_weight: bfloat16 [8192, 28672], P('blk', 'rows'), may hold values from -0.0625 to 0.0625
- down_weight: bfloat16 [28672, 8192], P('rows', 'blk'), may hold values from -0.03125 to 0.03125
Outputs:
- attended: bfloat16 [128, 4, 8192], P('rows', None, 'blk')
- layer_out: bfloat16 [128, 4, 8192], P('rows', None, 'blk')
Inputs may be any that keep to these rules, and one draw needn't show every extreme that they name: `swap_dest`: every owner sends exactly 2 of its pages to each of 32 different owners (possibly itself), and every owner receives exactly 64 pages. `page_table`: the entries of the 2 rows of one owner name each of its 64 resident pages and each of the 64 pages that land there exactly once; an entry at or above 64 is 64 + s * 2 + k for the k-th page, in the order of the sender's pages, that owner s sends to the row's owner. `lengths`: some row has exactly 1024 cached positions.
All inputs are finite; a program needn't handle non-finite values.
Results may differ from a plain program's by a relative error of at most 0.0086.
Values may be sent and summed in bfloat16 or wider, within the bound.
No kernel may reach another device: no remote copies, remote signals or barrier semaphores. Data moves between devices by JAX's collectives and lax.ppermute only.
A program may use at most 64 MiB of HBM per device.

v0:
```python
import math
import jax
import jax.numpy as jnp
from jax import lax
from jax.sharding import PartitionSpec as P

GQ = 8
HD = 128
PAGE = 16
CAP = 2
epsilon = 1e-05


def on_device(
    queries,
    new_entries,
    resident,
    swap_area,
    swap_dest,
    page_table,
    lengths,
    norm_gain,
    gate_weight,
    up_weight,
    down_weight,
):
    owners = lax.axis_size("rows")
    swap_count = swap_area.shape[0]
    page_width = swap_area.shape[1] * swap_area.shape[2] * swap_area.shape[3]
    flat_swap = swap_area.reshape(swap_count, page_width)
    target = swap_dest[:, None] == jnp.arange(owners, dtype=jnp.int32)[None, :]
    before = jnp.cumsum(target.astype(jnp.int32), axis=0) - 1
    page_rank = jnp.sum(jnp.where(target, before, 0), axis=1)
    send_slot = swap_dest * CAP + page_rank
    placement = (jnp.arange(owners * CAP, dtype=jnp.int32)[:, None] == send_slot[None, :]).astype(
        jnp.bfloat16
    )
    outgoing = jnp.dot(placement, flat_swap, preferred_element_type=jnp.float32).astype(
        jnp.bfloat16
    )
    outgoing = outgoing.reshape(owners, CAP, page_width)
    arrived = lax.all_to_all(outgoing, "rows", split_axis=0, concat_axis=0, tiled=True)
    page_store = jnp.concatenate(
        [resident.reshape(-1, page_width), arrived.reshape(owners * CAP, page_width)], axis=0
    )
    fetched = page_store[page_table]
    rows_here, pages_row = page_table.shape
    step_count = queries.shape[1]
    kv_heads = new_entries.shape[-1] // HD
    fetched = fetched.reshape(rows_here, pages_row, 2, PAGE, kv_heads, HD)
    cached_keys = fetched[:, :, 0].reshape(rows_here, pages_row * PAGE, kv_heads, HD)
    cached_values = fetched[:, :, 1].reshape(rows_here, pages_row * PAGE, kv_heads, HD)
    head_queries = queries.reshape(rows_here, step_count, kv_heads, GQ, HD)
    step_entries = new_entries.reshape(rows_here, step_count, 2, kv_heads, HD)
    score_scale = 1.0 / math.sqrt(HD)
    cached_scores = (
        jnp.einsum(
            "rskgd,rlkd->rkgsl", head_queries, cached_keys, preferred_element_type=jnp.float32
        )
        * score_scale
    )
    new_scores = (
        jnp.einsum(
            "rskgd,rtkd->rkgst",
            head_queries,
            step_entries[:, :, 0],
            preferred_element_type=jnp.float32,
        )
        * score_scale
    )
    visible = jnp.arange(pages_row * PAGE, dtype=jnp.int32)[None, :] < lengths[:, None]
    causal = jnp.arange(step_count)[None, :] <= jnp.arange(step_count)[:, None]
    cached_scores = jnp.where(visible[:, None, None, None, :], cached_scores, -1e30)
    new_scores = jnp.where(causal[None, None, None], new_scores, -1e30)
    row_peak = jnp.maximum(jnp.max(cached_scores, axis=-1), jnp.max(new_scores, axis=-1))[..., None]
    cached_exp = jnp.exp(cached_scores - row_peak)
    new_exp = jnp.exp(new_scores - row_peak)
    row_total = (jnp.sum(cached_exp, axis=-1) + jnp.sum(new_exp, axis=-1))[..., None]
    cached_weights = (cached_exp / row_total).astype(jnp.bfloat16)
    new_weights = (new_exp / row_total).astype(jnp.bfloat16)
    mixed_heads = jnp.einsum(
        "rkgsl,rlkd->rskgd", cached_weights, cached_values, preferred_element_type=jnp.float32
    )
    mixed_heads = mixed_heads + jnp.einsum(
        "rkgst,rtkd->rskgd", new_weights, step_entries[:, :, 1], preferred_element_type=jnp.float32
    )
    attended = mixed_heads.reshape(rows_here, step_count, -1).astype(jnp.bfloat16)
    local_tokens = attended.reshape(rows_here * step_count, -1)
    gathered = lax.all_gather(local_tokens, "rows", axis=0, tiled=True)
    gathered_wide = gathered.astype(jnp.float32)
    squares = jnp.sum(gathered_wide * gathered_wide, axis=1)
    normed = (gathered_wide * norm_gain.astype(jnp.float32)[None, :]).astype(jnp.bfloat16)
    gate_part = jnp.dot(normed, gate_weight, preferred_element_type=jnp.float32)
    up_part = jnp.dot(normed, up_weight, preferred_element_type=jnp.float32)
    width_total = gathered.shape[1] * lax.axis_size("blk")
    gate_sum, up_sum, square_sum = lax.psum((gate_part, up_part, squares), "blk")
    factor = lax.rsqrt(square_sum / width_total + epsilon)[:, None]
    hidden = (jax.nn.silu(factor * gate_sum) * (factor * up_sum)).astype(jnp.bfloat16)
    down_sum = lax.psum_scatter(
        jnp.dot(hidden, down_weight, preferred_element_type=jnp.float32),
        "rows",
        scatter_dimension=0,
        tiled=True,
    )
    layer_out = (local_tokens.astype(jnp.float32) + down_sum).astype(jnp.bfloat16)
    return (attended, layer_out.reshape(rows_here, step_count, -1))


def solution(mesh):
    placed = (
        P("rows", None, "blk"),
        P("rows", None, None, "blk"),
        P("rows", None, None, "blk"),
        P("rows", None, None, "blk"),
        P("rows"),
        P("rows", None),
        P("rows"),
        P("blk"),
        P("blk", "rows"),
        P("blk", "rows"),
        P("rows", "blk"),
    )
    return jax.shard_map(
        on_device,
        mesh=mesh,
        in_specs=placed,
        out_specs=(P("rows", None, "blk"), P("rows", None, "blk")),
        check_vma=False,
    )
```

profile of v0, /device:TPU:2, one launch (start us, length us, event | category | flops | bytes accessed | tf_op | source)
XLA Modules:
  0.0 548.7 jit_solution(16742943073197080970)
XLA Ops:
  7.2 0.8 fusion.23
  8.1 0.8 select_reduce_fusion
  8.9 0.7 multiply_add_fusion
  9.6 1.5 convolution_convert_fusion
  11.1 1.5 reshape.143
  12.6 18.9 %all-to-all-start = ((bf16[64,2,4096]{2,1,0:T(2,128)(2,1)}), bf16[64,2,4096]{2,1,0:T(2,128)(2,1)S(1)}, u32[]{:S(2)}, u32[]{:S(2)}) async-start(bf16[64,2,4096]{2,1,0:T(2,128)(2,1)} %reshape.143), calls=%async_computation | async-start | bytes 2097152 | tf_op jit(solution)/shard_map/all_to_all | solution.py:42
  31.7 1.0 copy.35
  32.7 0.6 pad_clamp_fusion
  33.3 0.7 iota_compare_fusion.3
  34.0 1.4 fusion.30
  35.4 52.2 %all-to-all-done = bf16[64,2,4096]{2,1,0:T(2,128)(2,1)S(1)} async-done(((bf16[64,2,4096]{2,1,0:T(2,128)(2,1)}), bf16[64,2,4096]{2,1,0:T(2,128)(2,1)S(1)}, u32[]{:S(2)}, u32[]{:S(2)}) %all-to-all-start) | async-done | bytes 1048608 | tf_op jit(solution)/shard_map/all_to_all | solution.py:42
  88.1 1.2 pad_maximum_fusion
  89.3 1.3 gather_fusion
  92.4 0.6 copy.36
  93.1 130.8 %all-gather.2.cloned.1.call-done = bf16[512,1024]{1,0:T(8,128)(2,1)} async-done(((bf16[8,1024]{1,0:T(8,128)(2,1)}), bf16[512,1024]{1,0:T(8,128)(2,1)}) %all-gather.2.cloned.1.call-update) | async-done | bytes 1048592 | tf_op jit(solution)/shard_map/all_gather | solution.py:89
  223.9 3.0 fusion.9
  226.9 2.8 fusion.11
  230.0 16.5 %psum.21 = f32[512]{0:T(512)S(1)} all-reduce(f32[512]{0:T(512)S(1)} %fusion), channel_id=1, replica_groups=mesh['blk'=8,'rows'=64] {'blk'}, use_global_device_ids=true, to_apply=%region_7.8 | all-reduce | flops 512 | bytes 4096 | tf_op jit(solution)/shard_map/psum | solution.py:96
  246.5 74.4 %all-reduce.3.cloned.1.call-done = (f32[512,448]{0,1:T(8,128)}, f32[512,448]{0,1:T(8,128)}) async-done(((f32[512,448]{0,1:T(8,128)}, f32[512,448]{0,1:T(8,128)}), (f32[512,448]{0,1:T(8,128)}, f32[512,448]{0,1:T(8,128)})) %all-reduce.3.cloned.1.call-update) | async-done | bytes 1835024 | tf_op jit(solution)/shard_map/psum | solution.py:96
  321.0 3.6 fusion.15
  324.6 0.6 convert_element_type.56
  325.2 215.6 %reduce-scatter.2.cloned.1.call-done = f32[8,1024]{1,0:T(8,128)} async-done(((f32[512,1024]{1,0:T(8,128)}), f32[8,1024]{1,0:T(8,128)}) %reduce-scatter.2.cloned.1.call-update) | async-done | bytes 32784 | tf_op jit(solution)/shard_map/reduce_scatter | solution.py:99
  540.8 0.8 add_convert_fusion
  541.6 0.6 reshape.154
  (53 shorter events, 2.8 us)
Async XLA Ops:
  7.2 313.8 %copy-start = (bf16[448,1024]{1,0:T(8,128)(2,1)S(1)}, bf16[448,1024]{1,0:T(8,128)(2,1)}, u32[]{:S(2)}) copy-start(bf16[448,1024]{1,0:T(8,128)(2,1)} %param.21) | copy-start | bytes 2752516
  11.1 20.5 %copy-start.11 = (s32[2,64]{1,0:T(2,128)S(1)}, s32[2,64]{1,0:T(2,128)}, u32[]{:S(2)}) copy-start(s32[2,64]{1,0:T(2,128)} %param.16) | copy-start | bytes 1540
  11.1 20.6 %copy-start.7 = (bf16[2,4,2,128]{3,2,1,0:T(2,128)(2,1)S(1)}, bf16[2,4,2,128]{3,2,1,0:T(2,128)(2,1)}, u32[]{:S(2)}) copy-start(bf16[2,4,2,128]{3,2,1,0:T(2,128)(2,1)} %param.12) | copy-start | bytes 12292
  11.1 20.6 %copy-start.5 = (bf16[2,4,1024]{2,1,0:T(4,128)(2,1)S(1)}, bf16[2,4,1024]{2,1,0:T(4,128)(2,1)}, u32[]{:S(2)}) copy-start(bf16[2,4,1024]{2,1,0:T(4,128)(2,1)} %param.11) | copy-start | bytes 49156
  11.1 20.6 %copy-start.2 = (bf16[64,2,16,128]{3,2,1,0:T(8,128)(2,1)S(1)}, bf16[64,2,16,128]{3,2,1,0:T(8,128)(2,1)}, u32[]{:S(2)}) copy-start(bf16[64,2,16,128]{3,2,1,0:T(8,128)(2,1)} %param.13) | copy-start | bytes 1572868
  12.6 20.7 %copy-start.12 = (s32[2]{0:T(128)S(1)}, s32[2]{0:T(128)}, u32[]{:S(2)}) copy-start(s32[2]{0:T(128)} %param.17) | copy-start | bytes 28
  12.6 75.0 %all-to-all-start = ((bf16[64,2,4096]{2,1,0:T(2,128)(2,1)}), bf16[64,2,4096]{2,1,0:T(2,128)(2,1)S(1)}, u32[]{:S(2)}, u32[]{:S(2)}) async-start(bf16[64,2,4096]{2,1,0:T(2,128)(2,1)} %reshape.143), calls=%async_computation | async-start | bytes 2097152 | tf_op jit(solution)/shard_map/all_to_all | solution.py:42
  31.5 192.4 %all-gather.2.cloned.1.call-start = ((), (), s32[]{:S(2)}) async-start(), calls=%async_computation.2 | async-start | bytes 1064960 | tf_op jit(solution)/shard_map/all_gather | solution.py:89
  31.7 3.7 copy-start.8
  90.6 0.7 copy-start.3
  90.6 1.0 copy-start.6
  90.6 1.0 copy-start.4
  90.9 1.3 copy-start.9
  90.9 2.2 copy-start.10
  90.9 133.0 %copy-start.13 = (bf16[1024,448]{0,1:T(8,128)(2,1)S(1)}, bf16[1024,448]{0,1:T(8,128)(2,1)}, u32[]{:S(2)}) copy-start(bf16[1024,448]{0,1:T(8,128)(2,1)} %param.20) | copy-start | bytes 2752516
  93.0 228.0 %all-reduce.3.cloned.1.call-start = ((), (), s32[]{:S(2)}) async-start(), calls=%async_computation.4 | async-start | bytes 3670016 | tf_op jit(solution)/shard_map/psum | solution.py:96
  223.9 3.0 copy-start.1
  229.7 311.1 %reduce-scatter.2.cloned.1.call-start = ((), (), s32[]{:S(2)}) async-start(), calls=%async_computation.3 | async-start | bytes 2129920 | tf_op jit(solution)/shard_map/reduce_scatter | solution.py:99
Sparse Core Ops, SparseCore 0:
  93.1 130.7 all-gather.1
  229.8 91.1 all-reduce.2
  325.6 215.1 reduce-scatter.1
where the time goes:
time: 549 us
  waiting for transfers between devices  473 us (86%)
  starting transfers between devices  19 us (3%)
  blocking collectives  16.5 us (3%)
  between operations  14 us (3%)
  matrix products  13.1 us (2%)
  local copies, waits for them, and re-layouts  6.88 us (1%)
  other arithmetic  6.15 us (1%)
    reduce_scatter x1, waiting for transfers between devices, on_device(): lax.psum_scatter(jnp.dot(hidden, down_weight, preferred_element_type=jnp....  216 us
    all_gather x1, waiting for transfers between devices, on_device(): gathered = lax.all_gather(local_tokens, 'rows', axis=0, tiled=True)  131 us
    psum x1, waiting for transfers between devices, on_device(): lax.psum((gate_part, up_part, squares), 'blk')  74.4 us
    all_to_all x1, waiting for transfers between devices, on_device(): lax.all_to_all(outgoing, 'rows', split_axis=0, concat_axis=0, tiled=True)  52.2 us
    all_to_all x1, starting transfers between devices, on_device(): lax.all_to_all(outgoing, 'rows', split_axis=0, concat_axis=0, tiled=True)  18.9 us
    psum x1, blocking collectives, on_device(): lax.psum((gate_part, up_part, squares), 'blk')  16.5 us
  transfers between devices with their start and end apart: 4, of which 4 were waited for; matrix products, arithmetic and copies ran while one was open for 1% of the time, Pallas kernels for 0%

commit v1 on v0

--- a/solution.py
+++ b/solution.py
@@ -86,7 +86,9 @@
     )
     attended = mixed_heads.reshape(rows_here, step_count, -1).astype(jnp.bfloat16)
     local_tokens = attended.reshape(rows_here * step_count, -1)
-    gathered = lax.all_gather(local_tokens, "rows", axis=0, tiled=True)
+    gathered = jnp.concatenate(
+        lax.all_to_all(jnp.stack([local_tokens] * lax.axis_size("rows")), "rows", 0, 0), axis=0
+    )
     gathered_wide = gathered.astype(jnp.float32)
     squares = jnp.sum(gathered_wide * gathered_wide, axis=1)
     normed = (gathered_wide * norm_gain.astype(jnp.float32)[None, :]).astype(jnp.bfloat16)

time: 549 us -> 474 us (0.86)
  the two profiles are of different devices: /device:TPU:2 before, /device:TPU:4 now
where the time goes in v1:
time: 474 us; the launch traced here: 473 us
  waiting for transfers between devices  394 us (83%)
  starting transfers between devices  24.2 us (5%)
  blocking collectives  15.8 us (3%)
  between operations  14.3 us (3%)
  matrix products  10.6 us (2%)
  local copies, waits for them, and re-layouts  7.53 us (2%)
  other arithmetic  6.16 us (1%)
    reduce_scatter x1, waiting for transfers between devices, on_device(): lax.psum_scatter(jnp.dot(hidden, down_weight, preferred_element_type=jnp....  216 us
    psum x1, waiting for transfers between devices, on_device(): lax.psum((gate_part, up_part, squares), 'blk')  69.8 us
    all_to_all x1, waiting for transfers between devices, on_device(): lax.all_to_all(jnp.stack([local_tokens] * lax.axis_size('rows')), 'rows',...  56.1 us
    all_to_all x1, waiting for transfers between devices, on_device(): lax.all_to_all(outgoing, 'rows', split_axis=0, concat_axis=0, tiled=True)  52.3 us
    all_to_all x1, starting transfers between devices, on_device(): lax.all_to_all(outgoing, 'rows', split_axis=0, concat_axis=0, tiled=True)  18.9 us
    psum x1, blocking collectives, on_device(): lax.psum((gate_part, up_part, squares), 'blk')  15.8 us
  transfers between devices with their start and end apart: 4, of which 4 were waited for; matrix products, arithmetic and copies ran while one was open for 1% of the time, Pallas kernels for 0%

profile of v1, /device:TPU:4, one launch (start us, length us, event | category | flops | bytes accessed | tf_op | source)
XLA Modules:
  0.0 473.0 jit_solution(3177475162041783183)
XLA Ops:
  7.2 0.8 fusion.24
  8.1 0.8 select_reduce_fusion
  8.9 0.7 multiply_add_fusion
  9.6 1.5 convolution_convert_fusion
  11.1 1.5 reshape.150
  12.6 18.9 %all-to-all-start = ((bf16[64,2,4096]{2,1,0:T(2,128)(2,1)}), bf16[64,2,4096]{2,1,0:T(2,128)(2,1)S(1)}, u32[]{:S(2)}, u32[]{:S(2)}) async-start(bf16[64,2,4096]{2,1,0:T(2,128)(2,1)} %reshape.150), calls=%async_computation | async-start | bytes 2097152 | tf_op jit(solution)/shard_map/all_to_all | solution.py:42
  31.7 1.0 copy.41
  33.3 0.7 iota_compare_fusion.3
  34.0 1.4 fusion.31
  35.3 52.3 %all-to-all-done = bf16[64,2,4096]{2,1,0:T(2,128)(2,1)S(1)} async-done(((bf16[64,2,4096]{2,1,0:T(2,128)(2,1)}), bf16[64,2,4096]{2,1,0:T(2,128)(2,1)S(1)}, u32[]{:S(2)}, u32[]{:S(2)}) %all-to-all-start) | async-done | bytes 1048608 | tf_op jit(solution)/shard_map/all_to_all | solution.py:42
  88.1 1.2 pad_maximum_fusion
  89.3 1.3 gather_fusion
  92.4 1.1 stack.3
  93.5 5.3 %all-to-all-start.1 = ((bf16[64,8,1024]{2,1,0:T(8,128)(2,1)}), bf16[64,8,1024]{2,1,0:T(8,128)(2,1)S(1)}, u32[]{:S(2)}, u32[]{:S(2)}) async-start(bf16[64,8,1024]{2,1,0:T(8,128)(2,1)} %stack.3), calls=%async_computation.1 | async-start | bytes 2097152 | tf_op jit(solution)/shard_map/all_to_all | solution.py:90
  98.9 56.1 %all-to-all-done.1 = bf16[64,8,1024]{2,1,0:T(8,128)(2,1)S(1)} async-done(((bf16[64,8,1024]{2,1,0:T(8,128)(2,1)}), bf16[64,8,1024]{2,1,0:T(8,128)(2,1)S(1)}, u32[]{:S(2)}, u32[]{:S(2)}) %all-to-all-start.1) | async-done | bytes 1048608 | tf_op jit(solution)/shard_map/all_to_all | solution.py:90
  155.0 1.6 fusion.10
  156.6 1.7 fusion.12
  158.7 15.8 %psum.21 = f32[512]{0:T(512)S(1)} all-reduce(f32[512]{0:T(512)S(1)} %reduce_sum.42), channel_id=1, replica_groups=mesh['blk'=8,'rows'=64] {'blk'}, use_global_device_ids=true, to_apply=%region_7.8 | all-reduce | flops 512 | bytes 4096 | tf_op jit(solution)/shard_map/psum | solution.py:98
  174.5 69.8 %all-reduce.3.cloned.1.call-done = (f32[512,448]{0,1:T(8,128)}, f32[512,448]{0,1:T(8,128)}) async-done(((f32[512,448]{0,1:T(8,128)}, f32[512,448]{0,1:T(8,128)}), (f32[512,448]{0,1:T(8,128)}, f32[512,448]{0,1:T(8,128)})) %all-reduce.3.cloned.1.call-update) | async-done | bytes 1835024 | tf_op jit(solution)/shard_map/psum | solution.py:98
  244.2 3.6 fusion.16
  247.9 0.6 convert_element_type.64
  248.5 216.4 %reduce-scatter.2.cloned.1.call-done = f32[8,1024]{1,0:T(8,128)} async-done(((f32[512,1024]{1,0:T(8,128)}), f32[8,1024]{1,0:T(8,128)}) %reduce-scatter.2.cloned.1.call-update) | async-done | bytes 32784 | tf_op jit(solution)/shard_map/reduce_scatter | solution.py:101
  464.8 0.8 add_convert_fusion
  465.6 0.6 reshape.161
  (54 shorter events, 3.5 us)
Async XLA Ops:
  7.2 237.0 %copy-start = (bf16[448,1024]{1,0:T(8,128)(2,1)S(1)}, bf16[448,1024]{1,0:T(8,128)(2,1)}, u32[]{:S(2)}) copy-start(bf16[448,1024]{1,0:T(8,128)(2,1)} %param.21) | copy-start | bytes 2752516
  11.1 20.4 %copy-start.10 = (s32[2,64]{1,0:T(2,128)S(1)}, s32[2,64]{1,0:T(2,128)}, u32[]{:S(2)}) copy-start(s32[2,64]{1,0:T(2,128)} %param.16) | copy-start | bytes 1540
  11.1 20.5 %copy-start.6 = (bf16[2,4,2,128]{3,2,1,0:T(2,128)(2,1)S(1)}, bf16[2,4,2,128]{3,2,1,0:T(2,128)(2,1)}, u32[]{:S(2)}) copy-start(bf16[2,4,2,128]{3,2,1,0:T(2,128)(2,1)} %param.12) | copy-start | bytes 12292
  11.1 20.5 %copy-start.4 = (bf16[2,4,1024]{2,1,0:T(4,128)(2,1)S(1)}, bf16[2,4,1024]{2,1,0:T(4,128)(2,1)}, u32[]{:S(2)}) copy-start(bf16[2,4,1024]{2,1,0:T(4,128)(2,1)} %param.11) | copy-start | bytes 49156
  11.1 20.5 %copy-start.1 = (bf16[64,2,16,128]{3,2,1,0:T(8,128)(2,1)S(1)}, bf16[64,2,16,128]{3,2,1,0:T(8,128)(2,1)}, u32[]{:S(2)}) copy-start(bf16[64,2,16,128]{3,2,1,0:T(8,128)(2,1)} %param.13) | copy-start | bytes 1572868
  12.6 20.7 %copy-start.11 = (s32[2]{0:T(128)S(1)}, s32[2]{0:T(128)}, u32[]{:S(2)}) copy-start(s32[2]{0:T(128)} %param.17) | copy-start | bytes 28
  12.6 75.0 %all-to-all-start = ((bf16[64,2,4096]{2,1,0:T(2,128)(2,1)}), bf16[64,2,4096]{2,1,0:T(2,128)(2,1)S(1)}, u32[]{:S(2)}, u32[]{:S(2)}) async-start(bf16[64,2,4096]{2,1,0:T(2,128)(2,1)} %reshape.150), calls=%async_computation | async-start | bytes 2097152 | tf_op jit(solution)/shard_map/all_to_all | solution.py:42
  31.6 3.7 copy-start.7
  90.6 0.7 copy-start.2
  90.6 1.0 copy-start.5
  90.6 1.0 copy-start.3
  90.9 1.3 copy-start.8
  91.9 7.0 %copy-start.9 = (bf16[1024]{0:T(1024)(128)(2,1)S(1)}, bf16[1024]{0:T(1024)(128)(2,1)}, u32[]{:S(2)}) copy-start(bf16[1024]{0:T(1024)(128)(2,1)} %param.18) | copy-start | bytes 6148
  91.9 63.1 %copy-start.12 = (bf16[1024,448]{0,1:T(8,128)(2,1)S(1)}, bf16[1024,448]{0,1:T(8,128)(2,1)}, u32[]{:S(2)}) copy-start(bf16[1024,448]{0,1:T(8,128)(2,1)} %param.20) | copy-start | bytes 2752516
  93.5 61.4 %all-to-all-start.1 = ((bf16[64,8,1024]{2,1,0:T(8,128)(2,1)}), bf16[64,8,1024]{2,1,0:T(8,128)(2,1)S(1)}, u32[]{:S(2)}, u32[]{:S(2)}) async-start(bf16[64,8,1024]{2,1,0:T(8,128)(2,1)} %stack.3), calls=%async_computation.1 | async-start | bytes 2097152 | tf_op jit(solution)/shard_map/all_to_all | solution.py:90
  98.8 145.4 %all-reduce.3.cloned.1.call-start = ((), (), s32[]{:S(2)}) async-start(), calls=%async_computation.4 | async-start | bytes 3670016 | tf_op jit(solution)/shard_map/psum | solution.py:98
  155.0 1.6 copy-start.13
  158.3 306.5 %reduce-scatter.2.cloned.1.call-start = ((), (), s32[]{:S(2)}) async-start(), calls=%async_computation.3 | async-start | bytes 2129920 | tf_op jit(solution)/shard_map/reduce_scatter | solution.py:101
Sparse Core Ops, SparseCore 0:
  158.4 85.7 all-reduce.2
  248.9 215.9 reduce-scatter.1
